TPU v7x, 512 devices: a whole 4x8x8 slice. The times are simulated.
512 devices in a mesh: head: 8 (over z), blk: 64 (over x, y, core).
Axes of the slice: x: 4, y: 8, z: 8, core: 2. Of those that a mesh axis runs over, the one named last changes fastest.
Arguments:
- vision: bfloat16 [4, 1408, 8192], P(None, 'head', 'blk'), may hold values from -600 to 600
- ln_gain: float32 [1408], P('head'), may hold values from 0.5 to 1.5
- merge_proj: bfloat16 [4, 1408, 1408], P(None, 'head'), may hold values from -0.078125 to 0.078125
- image_slot: int32 [2048], P('blk'), may hold values from 0 to 32764, as said below
- text: bfloat16 [1408, 32768], P('head', 'blk'), may hold values from -600 to 600
- rms_gain: float32 [1408], replicated, may hold values from 0.5 to 1.5
- wqkv: bfloat16 [3, 1408, 1408], P(None, 'head'), may hold values from -0.31835938 to 0.31835938
- pcache: bfloat16 [2, 1408, 131072], P(None, 'head', 'blk'), may hold values from -300 to 300
- block_table: int32 [64, 128], replicated, may hold values from -1 to 4095, as said below
- cache_len: int32 [64], P('blk'), may hold values from 1 to 4096, as said below
Outputs:
- attended: bfloat16 [1408, 32768], P('head', 'blk')
- new_cache: bfloat16 [2, 1408, 32768], P(None, 'head', 'blk')
Inputs may be any that keep to these rules, and one draw needn't show every extreme that they name: `image_slot`: pieces never intersect and start at multiples of 4; the 32 pieces held by one index of blk start in the rows of 32 different requests, and every request receives exactly 32 pieces. `block_table`: row r holds a block number for j < ceil(cache_len[r] / 32) and -1 after; no block number appears twice; index d of blk holds blocks d * 64 to (d+1) * 64 - 1. The longest request has exactly 2 blocks on every index of blk; every other request has at most one block on any index. `cache_len`: exactly one request, the longest, has 4096 cached positions; all others have fewer.
All inputs are finite; a program needn't handle non-finite values.
Results may differ from a plain program's by a relative error of at most 0.025.
The roundings to bfloat16 on the way count: a program that leaves them out, or rounds other values in their place, can miss the bound.
Values may be sent and summed in bfloat16 or wider, within the bound.
A program may use at most 128 MiB of HBM per device.

v0:
```python
import math
import jax
import jax.numpy as jnp
from jax import lax
from jax.sharding import PartitionSpec as P

D = 1408
HD = 88
BS = 32
masked_score = -1e30


def rotary_columns(values, places):
    half = values.shape[1] // 2
    freq_index = jnp.arange(half, dtype=jnp.float32)
    inverse = jnp.exp(freq_index * (-2.0 * math.log(10000.0) / values.shape[1]))
    angles = inverse[:, None] * places[None, :]
    cosine = jnp.cos(angles)[None]
    sine_part = jnp.sin(angles)[None]
    leading = values[:, :half]
    trailing = values[:, half:]
    return jnp.concatenate(
        [leading * cosine - trailing * sine_part, trailing * cosine + leading * sine_part], axis=1
    )


def softmax_part(query_block, keys, values, mask, scale):
    scores = (
        jnp.einsum("hdq,hdk->hqk", query_block, keys, preferred_element_type=jnp.float32) * scale
    )
    scores = jnp.where(mask[None], scores, masked_score)
    highest = jnp.max(scores, axis=2)
    expo = jnp.where(mask[None], jnp.exp(scores - highest[:, :, None]), 0.0)
    total = jnp.sum(expo, axis=2)
    mixed = jnp.einsum("hqk,hdk->hdq", expo, values, precision=lax.Precision.HIGHEST)
    return (mixed, highest, total)


def fold_softmax(first, second):
    mixed_a, high_a, total_a = first
    mixed_b, high_b, total_b = second
    top = jnp.maximum(high_a, high_b)
    factor_a = jnp.exp(high_a - top)
    factor_b = jnp.exp(high_b - top)
    return (
        mixed_a * factor_a[:, None, :] + mixed_b * factor_b[:, None, :],
        top,
        total_a * factor_a + total_b * factor_b,
    )


def unblock(parts):
    mixed, highest, total = parts
    heads_here = mixed.shape[1]
    mixed = jnp.transpose(mixed, (1, 2, 0, 3)).reshape(heads_here, mixed.shape[2], -1)
    highest = jnp.transpose(highest, (1, 0, 2)).reshape(heads_here, -1)
    total = jnp.transpose(total, (1, 0, 2)).reshape(heads_here, -1)
    return (mixed, highest, total)


def shards(
    vision, ln_gain, merge_proj, image_slot, text, rms_gain, wqkv, pcache, block_table, cache_len
):
    local = vision.shape[1]
    groups = vision.shape[2]
    floats = vision.astype(jnp.float32)
    totals, squares = lax.psum((jnp.sum(floats, axis=1), jnp.sum(floats * floats, axis=1)), "head")
    average = totals / D
    spread = squares / D - average * average
    normed_vision = (
        (floats - average[:, None, :])
        * lax.rsqrt(spread + 1e-06)[:, None, :]
        * ln_gain[None, :, None]
    ).astype(jnp.bfloat16)
    partial_rows = jnp.einsum(
        "tcd,tcg->dg", merge_proj, normed_vision, preferred_element_type=jnp.float32
    )
    merged_columns = lax.psum_scatter(partial_rows, "head", scatter_dimension=0, tiled=True).astype(
        jnp.bfloat16
    )
    merged = jnp.transpose(merged_columns)
    devices = lax.axis_size("blk")
    here = lax.axis_index("blk")
    rows_here = text.shape[1]
    pieces = image_slot.shape[0]
    piece_rows = groups // pieces
    lines = jnp.arange(rows_here, dtype=jnp.int32)
    offsets = jnp.arange(piece_rows, dtype=jnp.int32)
    target = image_slot // rows_here
    within = image_slot % rows_here
    select = target[None, :] == jnp.arange(devices, dtype=jnp.int32)[:, None]
    outbound = (
        jnp.dot(
            select.astype(jnp.bfloat16),
            merged.reshape(pieces, piece_rows * local),
            preferred_element_type=jnp.float32,
        )
        .astype(jnp.bfloat16)
        .reshape(devices, piece_rows, local)
    )
    starts = jnp.sum(jnp.where(select, within[None, :] + 1, 0), axis=1) - 1
    arrived, arrived_start = (
        lax.all_to_all(outbound, "blk", split_axis=0, concat_axis=0, tiled=True),
        lax.all_to_all(starts, "blk", split_axis=0, concat_axis=0, tiled=True),
    )
    row_ids = (arrived_start[:, None] + offsets[None, :]).reshape(-1)
    present = jnp.repeat(arrived_start >= 0, piece_rows)
    hits = (row_ids[:, None] == lines[None, :]) & present[:, None]
    placed_rows = jnp.einsum(
        "kl,kr->lr",
        arrived.reshape(devices * piece_rows, local),
        hits.astype(jnp.bfloat16),
        preferred_element_type=jnp.float32,
    ).astype(jnp.bfloat16)
    covered = jnp.any(hits, axis=0)
    placed = jnp.where(covered[None, :], placed_rows, text)
    row_floats = placed.astype(jnp.float32)
    square_sums = lax.psum(jnp.sum(row_floats * row_floats, axis=0), "head")
    gain_here = lax.dynamic_slice_in_dim(rms_gain, lax.axis_index("head") * local, local)
    normed = (row_floats * lax.rsqrt(square_sums / D + 1e-06)[None, :] * gain_here[:, None]).astype(
        jnp.bfloat16
    )
    projected = jnp.einsum(
        "jod,dr->jor",
        wqkv,
        lax.all_gather(normed, "head", axis=0, tiled=True),
        preferred_element_type=jnp.float32,
    )
    heads_here = local // HD
    projected = projected.reshape(3, heads_here, HD, rows_here)
    places = (cache_len[0] + lines).astype(jnp.float32)
    queries = rotary_columns(projected[0], places).astype(jnp.bfloat16)
    new_keys = rotary_columns(projected[1], places).astype(jnp.bfloat16)
    new_values = projected[2].astype(jnp.bfloat16)
    new_cache = jnp.stack(
        [new_keys.reshape(local, rows_here), new_values.reshape(local, rows_here)], axis=0
    )
    block_len = BS
    owned = pcache.shape[2] // block_len
    paged = pcache.reshape(2, local, owned, block_len)
    requests = block_table.shape[0]
    table_width = block_table.shape[1]
    slots_each = table_width // devices
    block_ids = here * owned + jnp.arange(owned, dtype=jnp.int32)
    matches = block_table[None, :, :] == block_ids[:, None, None]
    found = jnp.any(matches, axis=2)
    in_use = jnp.any(found, axis=1)
    owner = jnp.sum(jnp.where(found, jnp.arange(requests, dtype=jnp.int32)[None, :], 0), axis=1)
    logical = jnp.sum(
        jnp.where(matches, jnp.arange(table_width, dtype=jnp.int32)[None, None, :], 0), axis=(1, 2)
    )
    counter = jnp.arange(owned, dtype=jnp.int32)
    earlier = (
        (owner[:, None] == owner[None, :]) & in_use[None, :] & (counter[None, :] < counter[:, None])
    )
    standing = jnp.sum(earlier.astype(jnp.int32), axis=1)
    within_block = jnp.arange(block_len, dtype=jnp.int32)
    block_rows = min(rows_here, 512)
    count_blocks = rows_here // block_rows
    scale = HD ** (-0.5)
    query_blocks = jnp.transpose(
        queries.reshape(heads_here, HD, count_blocks, block_rows), (2, 0, 1, 3)
    )
    first_rows = jnp.arange(count_blocks, dtype=jnp.int32) * block_rows
    destination = owner * slots_each + standing
    routing = (destination[None, :] == jnp.arange(table_width, dtype=jnp.int32)[:, None]) & in_use[
        None, :
    ]
    outgoing = jnp.einsum(
        "wo,cfob->cfwb", routing.astype(jnp.bfloat16), paged, preferred_element_type=jnp.float32
    ).astype(jnp.bfloat16)
    outgoing = outgoing.reshape(2, local, table_width * block_len)
    labels = jnp.sum(jnp.where(routing, logical[None, :] + 1, 0), axis=1) - 1
    labels = labels.reshape(1, 1, table_width)
    blocks_in, labels_in = (
        lax.all_to_all(outgoing, "blk", split_axis=2, concat_axis=2, tiled=True),
        lax.all_to_all(labels, "blk", split_axis=2, concat_axis=2, tiled=True),
    )
    cached_keys = blocks_in[0].reshape(heads_here, HD, -1)
    cached_values = blocks_in[1].reshape(heads_here, HD, -1).astype(jnp.float32)
    label_flat = labels_in.reshape(-1)
    key_places = label_flat[:, None] * block_len + within_block[None, :]
    live = ((label_flat[:, None] >= 0) & (key_places < cache_len[0])).reshape(-1)
    old_mask = jnp.broadcast_to(live[None, :], (block_rows, live.shape[0]))
    new_values_f = new_values.astype(jnp.float32)

    def attend(inputs):
        query_block, first_row = inputs
        causal = (first_row + jnp.arange(block_rows, dtype=jnp.int32))[:, None] >= lines[None, :]
        old_part = softmax_part(query_block, cached_keys, cached_values, old_mask, scale)
        own_part = softmax_part(query_block, new_keys, new_values_f, causal, scale)
        return fold_softmax(old_part, own_part)

    mixed, highest, total = unblock(lax.map(attend, (query_blocks, first_rows)))
    attended = (mixed / total[:, None, :]).astype(jnp.bfloat16).reshape(local, rows_here)
    return (attended, new_cache)


def solution(mesh):
    in_specs = (
        P(None, "head", "blk"),
        P("head"),
        P(None, "head", None),
        P("blk"),
        P("head", "blk"),
        P(),
        P(None, "head", None),
        P(None, "head", "blk"),
        P(),
        P("blk"),
    )
    out_specs = (P("head", "blk"), P(None, "head", "blk"))
    return jax.shard_map(shards, mesh=mesh, in_specs=in_specs, out_specs=out_specs, check_vma=False)
```

profile of v0, /device:TPU:1, one launch (start us, length us, event | category | flops | bytes accessed | tf_op | source)
XLA Modules:
  0.0 288.2 jit_solution(1287686254156349032)
XLA Ops:
  8.3 20.3 %all-reduce = (f32[4,128]{1,0:T(4,128)S(1)}, f32[4,128]{1,0:T(4,128)S(1)}) all-reduce(f32[4,128]{1,0:T(4,128)S(1)} %get-tuple-element.23, f32[4,128]{1,0:T(4,128)S(1)} %get-tuple-element.22), channel_id=1, replica_groups=mesh['head'=8,'blk'=64] {'head'}, use_global_device_ids=true, to_apply=%region_11.12 | all-reduce | flops 1024 | bytes 8192 | tf_op jit(solution)/shard_map/psum | solution.py:67
  32.2 14.5 %all-to-all-start.2 = ((s32[64,1,1]{2,1,0:T(1,128)}), s32[64,1,1]{2,1,0:T(1,128)S(1)}, u32[]{:S(2)}, u32[]{:S(2)}) async-start(s32[64,1,1]{2,1,0:T(1,128)} %copy.44), calls=%async_computation.2 | async-start | bytes 65536 | tf_op jit(solution)/shard_map/all_to_all | solution.py:104
  46.8 2.4 compare_reduce_fusion
  51.7 3.7 %copy.38 = bf16[2,176,2048]{1,2,0:T(8,128)(2,1)} copy(bf16[2,176,2048]{2,1,0:T(8,128)(2,1)} %param.17) | data formatting | bytes 2883584 | tf_op args[7]
  55.4 13.9 %reduce-scatter.4.cloned.1.call-done = f32[176,128]{1,0:T(8,128)} async-done(((f32[1408,128]{1,0:T(8,128)}), f32[176,128]{1,0:T(8,128)}) %reduce-scatter.4.cloned.1.call-update) | async-done | bytes 90128
  70.4 14.6 %all-to-all-start.1 = ((s32[1,1,128]{1,0,2:T(1,128)}), s32[1,1,128]{1,0,2:T(1,128)S(1)}, u32[]{:S(2)}, u32[]{:S(2)}) async-start(s32[1,1,128]{1,0,2:T(1,128)} %copy.43), calls=%async_computation.1 | async-start | bytes 131072 | tf_op jit(solution)/shard_map/all_to_all | solution.py:177
  86.1 8.7 %all-to-all-done.1 = s32[1,1,128]{1,0,2:T(1,128)S(1)} async-done(((s32[1,1,128]{1,0,2:T(1,128)}), s32[1,1,128]{1,0,2:T(1,128)S(1)}, u32[]{:S(2)}, u32[]{:S(2)}) %all-to-all-start.1) | async-done | bytes 544 | tf_op jit(solution)/shard_map/all_to_all | solution.py:177
  94.8 4.4 %all-to-all-start.3 = ((bf16[64,4,176]{2,1,0:T(4,128)(2,1)}), bf16[64,4,176]{2,1,0:T(4,128)(2,1)S(1)}, u32[]{:S(2)}, u32[]{:S(2)}) async-start(bf16[64,4,176]{2,1,0:T(4,128)(2,1)} %reshape.266), calls=%async_computation.3 | async-start | bytes 262144 | tf_op jit(solution)/shard_map/all_to_all | solution.py:103
  99.2 4.9 %convert_bitcast_fusion = bf16[2,176,128,32]{2,1,3,0:T(8,128)(2,1)} fusion(bf16[2,176,64,32]{1,3,2,0:T(8,128)(2,1)} %bitcast.47, s32[64]{0:T(128)S(1)} %get-tuple-element.61, pred[64]{0:T(512)(128)(4,1)S(1)} %get-tuple-element.24), kind=kOutput, calls=%fused_computation.13 | convolution fusion | flops 186007552 | bytes 4325696 | tf_op jit(solution)/shard_map/wo,cfob->cfwb/dot_general | solution.py:169
  104.1 7.7 %copy.40 = bf16[2,176,128,32]{1,3,2,0:T(8,128)(2,1)} copy(bf16[2,176,128,32]{2,1,3,0:T(8,128)(2,1)} %convert_bitcast_fusion) | data formatting | bytes 5767168 | tf_op jit(solution)/shard_map/convert_element_type | solution.py:171
  111.8 10.1 %copy.41 = bf16[2,176,4096]{1,0,2:T(2,128)(2,1)} copy(bf16[2,176,4096]{1,2,0:T(8,128)(2,1)} %bitcast.46) | data formatting | bytes 5767168 | tf_op jit(solution)/shard_map/reshape | solution.py:172
  121.9 10.8 %all-to-all-start = ((bf16[2,176,4096]{1,0,2:T(2,128)(2,1)}), bf16[2,176,4096]{1,0,2:T(2,128)(2,1)}, u32[]{:S(2)}, u32[]{:S(2)}) async-start(bf16[2,176,4096]{1,0,2:T(2,128)(2,1)} %copy.41), calls=%async_computation | async-start | bytes 8388608 | tf_op jit(solution)/shard_map/all_to_all | solution.py:176
  135.7 13.1 %psum.23 = f32[512]{0:T(512)S(1)} all-reduce(f32[512]{0:T(512)S(1)} %get-tuple-element.55), channel_id=1, replica_groups=mesh['head'=8,'blk'=64] {'head'}, use_global_device_ids=true, to_apply=%region_14.15 | all-reduce | flops 512 | bytes 4096 | tf_op jit(solution)/shard_map/psum | solution.py:118
  150.9 2.4 multiply_reduce_fusion.1
  153.2 2.4 compare_reduce_fusion.2
  155.8 34.9 %all-gather.2.cloned.1.call-done = bf16[1408,512]{1,0:T(8,128)(2,1)} async-done(((bf16[176,512]{1,0:T(8,128)(2,1)}), bf16[1408,512]{1,0:T(8,128)(2,1)}) %all-gather.2.cloned.1.call-update) | async-done | bytes 1441808 | tf_op jit(solution)/shard_map/all_gather | solution.py:126
  190.7 2.8 fusion.15
  197.2 31.4 %all-to-all-done = bf16[2,176,4096]{1,0,2:T(2,128)(2,1)} async-done(((bf16[2,176,4096]{1,0,2:T(2,128)(2,1)}), bf16[2,176,4096]{1,0,2:T(2,128)(2,1)}, u32[]{:S(2)}, u32[]{:S(2)}) %all-to-all-start) | async-done | bytes 2883616 | tf_op jit(solution)/shard_map/all_to_all | solution.py:176
  228.6 9.8 %fusion.66 = (bf16[1,176,4096]{1,0,2:T(2,128)(2,1)}, bf16[1,176,4096]{1,0,2:T(2,128)(2,1)}) fusion(bf16[2,176,4096]{1,0,2:T(2,128)(2,1)} %all-to-all-done), kind=kLoop, calls=%fused_computation.118 | loop fusion | bytes 5767168 | tf_op jit(solution)/shard_map/slice | solution.py:180
  238.3 9.6 %copy.42 = bf16[1,176,4096]{2,1,0:T(8,128)(2,1)} copy(bf16[1,176,4096]{1,0,2:T(2,128)(2,1)} %get-tuple-element.41) | data formatting | bytes 2883584 | tf_op jit(solution)/shard_map/slice | solution.py:180
  247.9 9.8 %copy.45 = bf16[1,176,4096]{2,1,0:T(8,128)(2,1)S(1)} copy(bf16[1,176,4096]{1,0,2:T(2,128)(2,1)} %get-tuple-element.42) | data formatting | bytes 2883584 | tf_op jit(solution)/shard_map/slice | solution.py:179
  257.7 3.7 %fusion = (f32[2,512]{1,0:T(2,128)S(1)}, f32[2,512,4096]{2,1,0:T(8,128)S(1)}) fusion(pred[4096]{0:T(1024)(128)(4,1)S(1)} %and.63, bf16[2,88,4096]{2,1,0:T(8,128)(2,1)S(1)} %bitcast.48, bf16[2,44,512]{2,1,0:T(8,128)(2,1)} %copy-done.8, bf16[2,44,512]{2,1,0:T(8,128)(2,1)S(1)} %get-tuple-element.45), kind=kOutput, calls=%fused_computation.2 | convolution fusion | flops 751139840 | bytes 18407424 | tf_op jit(solution)/shard_map/while/body/eval_jaxpr/hdq,hdk->hqk/dot_general | solution.py:29
  261.5 5.1 %fusion.1 = f32[2,512]{1,0:T(2,128)S(1)} fusion(f32[2,512,4096]{2,1,0:T(8,128)S(1)} %get-tuple-element.60, f32[2,512]{1,0:T(2,128)S(1)} %get-tuple-element.59, pred[4096]{0:T(1024)(128)(4,1)S(1)} %and.63), kind=kLoop, calls=%fused_computation.3 | loop fusion | flops 20970496 | bytes 16789504 | tf_op jit(solution)/shard_map/while/body/eval_jaxpr/reduce_sum | solution.py:34
  268.1 13.2 %fusion.29 = bf16[2,88,512]{2,1,0:T(8,128)(2,1)} fusion(f32[2,88,512]{2,1,0:T(8,128)S(1)} %fusion.20, bf16[2,88,4096]{2,1,0:T(8,128)(2,1)S(1)} %bitcast.51, f32[2,512,4096]{2,1,0:T(8,128)S(1)} %get-tuple-element.60, f32[2,512]{1,0:T(2,128)S(1)} %get-tuple-element.59, pred[4096]{0:T(1024)(128)(4,1)S(1)} %and.63, f32[2,512]{1,0:T(2,128)S(1)} %get-tuple-element.28, ...), kind=kOutput, calls=%fused_computation.39 | convolution fusion | flops 4446322688 | bytes 18776064 | tf_op jit(solution)/shard_map/while/body/eval_jaxpr/hqk,hdk->hdq/dot_general | solution.py:35
  (78 shorter events, 19.1 us)
Async XLA Ops:
  7.2 21.5 %copy-start = (bf16[4,176,1408]{2,1,0:T(8,128)(2,1)S(1)}, bf16[4,176,1408]{2,1,0:T(8,128)(2,1)}, u32[]{:S(2)}) copy-start(bf16[4,176,1408]{2,1,0:T(8,128)(2,1)} %param.12) | copy-start | bytes 5947396
  7.2 62.0 %reduce-scatter.4.cloned.1.call-start = ((), (), s32[]{:S(2)}) async-start(), calls=%async_computation.6 | async-start | bytes 811008
  28.6 2.7 copy-start.11
  28.6 18.1 %copy-start.9 = (s32[64,128]{1,0:T(8,128)S(1)}, s32[64,128]{1,0:T(8,128)}, u32[]{:S(2)}) copy-start(s32[64,128]{1,0:T(8,128)} %param.18) | copy-start | bytes 98308
  32.2 38.2 %all-to-all-start.2 = ((s32[64,1,1]{2,1,0:T(1,128)}), s32[64,1,1]{2,1,0:T(1,128)S(1)}, u32[]{:S(2)}, u32[]{:S(2)}) async-start(s32[64,1,1]{2,1,0:T(1,128)} %copy.44), calls=%async_computation.2 | async-start | bytes 65536 | tf_op jit(solution)/shard_map/all_to_all | solution.py:104
  70.4 24.4 %all-to-all-start.1 = ((s32[1,1,128]{1,0,2:T(1,128)}), s32[1,1,128]{1,0,2:T(1,128)S(1)}, u32[]{:S(2)}, u32[]{:S(2)}) async-start(s32[1,1,128]{1,0,2:T(1,128)} %copy.43), calls=%async_computation.1 | async-start | bytes 131072 | tf_op jit(solution)/shard_map/all_to_all | solution.py:177
  94.8 27.1 %all-to-all-start.3 = ((bf16[64,4,176]{2,1,0:T(4,128)(2,1)}), bf16[64,4,176]{2,1,0:T(4,128)(2,1)S(1)}, u32[]{:S(2)}, u32[]{:S(2)}) async-start(bf16[64,4,176]{2,1,0:T(4,128)(2,1)} %reshape.266), calls=%async_computation.3 | async-start | bytes 262144 | tf_op jit(solution)/shard_map/all_to_all | solution.py:103
  121.9 13.5 %copy-start.10 = (bf16[176,512]{1,0:T(8,128)(2,1)S(1)}, bf16[176,512]{1,0:T(8,128)(2,1)}, u32[]{:S(2)}) copy-start(bf16[176,512]{1,0:T(8,128)(2,1)} %param.14) | copy-start | bytes 540676
  121.9 106.7 %all-to-all-start = ((bf16[2,176,4096]{1,0,2:T(2,128)(2,1)}), bf16[2,176,4096]{1,0,2:T(2,128)(2,1)}, u32[]{:S(2)}, u32[]{:S(2)}) async-start(bf16[2,176,4096]{1,0,2:T(2,128)(2,1)} %copy.41), calls=%async_computation | async-start | bytes 8388608 | tf_op jit(solution)/shard_map/all_to_all | solution.py:176
  132.7 58.0 %all-gather.2.cloned.1.call-start = ((), (), s32[]{:S(2)}) async-start(), calls=%async_computation.5 | async-start | bytes 1622016 | tf_op jit(solution)/shard_map/all_gather | solution.py:126
  150.5 44.8 %copy-start.4 = (pred[512,512]{0,1:T(8,128)(4,1)}, pred[512,512]{0,1:T(8,128)(4,1)S(1)}, u32[]{:S(2)}) copy-start(pred[512,512]{0,1:T(8,128)(4,1)S(1)} %iota_compare_fusion) | copy-start | bytes 786436
  193.6 1.0 copy-start.6
  194.6 2.6 copy-start.8
  195.2 1.4 copy-start.1
  261.4 5.2 %copy-start.2 = (f32[2,512,512]{1,2,0:T(8,128)S(1)}, f32[2,512,512]{1,2,0:T(8,128)}, u32[]{:S(2)}) copy-start(f32[2,512,512]{1,2,0:T(8,128)} %copy-done.1) | copy-start | bytes 6291460
  261.5 5.2 %copy-start.5 = (pred[512,512]{0,1:T(8,128)(4,1)S(1)}, pred[512,512]{0,1:T(8,128)(4,1)}, u32[]{:S(2)}) copy-start(pred[512,512]{0,1:T(8,128)(4,1)} %copy-done.4) | copy-start | bytes 786436
  261.5 5.2 %copy-start.7 = (bf16[1,176,512]{2,1,0:T(8,128)(2,1)S(1)}, bf16[1,176,512]{2,1,0:T(8,128)(2,1)}, u32[]{:S(2)}) copy-start(bf16[1,176,512]{2,1,0:T(8,128)(2,1)} %copy-done.6) | copy-start | bytes 540676
  266.6 1.5 copy-start.3
Sparse Core Ops, SparseCore 0:
  31.5 37.7 reduce-scatter.3
  149.8 40.8 all-gather.1
where the time goes:
time: 290 us; the launch traced here: 288 us
  waiting for transfers between devices  88.9 us (31%)
  local copies, waits for them, and re-layouts  57.9 us (20%)
  starting transfers between devices  44.4 us (15%)
  blocking collectives  33.4 us (12%)
  matrix products  28.9 us (10%)
  other arithmetic  19.6 us (7%)
  between operations  15.1 us (5%)
    all_gather x1, waiting for transfers between devices, shards(): lax.all_gather(normed, 'head', axis=0, tiled=True)  34.9 us
    all_to_all x1, waiting for transfers between devices, shards(): lax.all_to_all(outgoing, 'blk', split_axis=2, concat_axis=2, tiled=True)  31.4 us
    psum x1, blocking collectives, shards(): lax.psum((jnp.sum(floats, axis=1), jnp.sum(floats * floats, axis=1)), 'he...  20.3 us
    slice x2, local copies, waits for them, and re-layouts, shards(): cached_values = blocks_in[1].reshape(heads_here, HD, -1).astype(jnp.float32)  19.4 us
    dot_general x2, matrix products, softmax_part(): jnp.einsum('hqk,hdk->hdq', expo, values, precision=lax.Precision.HIGHEST)  14.7 us
    all_to_all x1, starting transfers between devices, shards(): lax.all_to_all(labels, 'blk', split_axis=2, concat_axis=2, tiled=True)  14.6 us
    all_to_all x1, starting transfers between devices, shards(): lax.all_to_all(starts, 'blk', split_axis=0, concat_axis=0, tiled=True)  14.5 us
    unnamed x3, waiting for transfers between devices  13.9 us
  transfers between devices with their start and end apart: 6, of which 4 were waited for; matrix products, arithmetic and copies ran while one was open for 17% of the time, Pallas kernels for 0%

commit v1 on v0

--- a/solution.py
+++ b/solution.py
@@ -8,6 +8,22 @@
 HD = 88
 BS = 32
 masked_score = -1e30
+
+
+def product_in_turn(shard, axis, dim, product):
+    devices, index, span = (lax.axis_size(axis), lax.axis_index(axis), shard.shape[dim])
+    right = [(i, (i + 1) % devices) for i in range(devices)]
+    left = [(i, (i - 1) % devices) for i in range(devices)]
+    half = devices // 2
+    from_left = from_right = shard
+    total = product(shard, index * span)
+    for step in range(1, half + 1):
+        from_left = lax.ppermute(from_left, axis, right)
+        if step < devices - half:
+            from_right = lax.ppermute(from_right, axis, left)
+            total = total + product(from_right, (index + step) % devices * span)
+        total = total + product(from_left, (index - step) % devices * span)
+    return total
 
 
 def rotary_columns(values, places):
@@ -120,11 +136,16 @@
     normed = (row_floats * lax.rsqrt(square_sums / D + 1e-06)[None, :] * gain_here[:, None]).astype(
         jnp.bfloat16
     )
-    projected = jnp.einsum(
-        "jod,dr->jor",
-        wqkv,
-        lax.all_gather(normed, "head", axis=0, tiled=True),
-        preferred_element_type=jnp.float32,
+    projected = product_in_turn(
+        normed,
+        "head",
+        0,
+        lambda part, offset: jnp.einsum(
+            "jod,dr->jor",
+            lax.dynamic_slice_in_dim(wqkv, offset, part.shape[0], axis=2),
+            part,
+            preferred_element_type=jnp.float32,
+        ),
     )
     heads_here = local // HD
     projected = projected.reshape(3, heads_here, HD, rows_here)

time: 290 us -> 283 us (0.976)
  waiting for transfers between devices: 88.9 us -> 70.7 us
  starting transfers between devices: 44.4 us -> 58.3 us
    all_gather x1 -> x0, waiting for transfers between devices: 34.9 us -> none  [shards(): lax.all_gather(normed, 'head', axis=0, tiled=True)]
    ppermute x0 -> x7, starting transfers between devices: none -> 21.4 us  [the longest x3 13.3 us: product_in_turn(): from_right = lax.ppermute(from_right, axis, left)]
    all_to_all x1, waiting for transfers between devices: 0.01 us -> 10.4 us  [shards(): lax.all_to_all(outbound, 'blk', split_axis=0, concat_axis=0, tiled=True)]
    unnamed x3 -> x2, waiting for transfers between devices: 13.9 us -> 5.51 us
    all_to_all x1, waiting for transfers between devices: 31.4 us -> 38.7 us  [shards(): lax.all_to_all(outgoing, 'blk', split_axis=2, concat_axis=2, tiled=True)]
    ppermute x0 -> x7, waiting for transfers between devices: none -> 7.31 us  [the longest x4 7.3 us: product_in_turn(): from_left = lax.ppermute(from_left, axis, right)]
    all_to_all x1, starting transfers between devices: 10.8 us -> 5.61 us  [shards(): lax.all_to_all(outgoing, 'blk', split_axis=2, concat_axis=2, tiled=True)]
    all_to_all x1, starting transfers between devices: 14.5 us -> 11.6 us  [shards(): lax.all_to_all(starts, 'blk', split_axis=0, concat_axis=0, tiled=True)]
  transfers between devices with their start and end apart: 6 -> 12, of which waited for: 4 -> 8; matrix products, arithmetic and copies ran while one was open for 17% -> 18% of each run, Pallas kernels for 0% -> 0%
where the time goes in v1:
time: 283 us; the launch traced here: 282 us
  waiting for transfers between devices  70.7 us (25%)
  starting transfers between devices  58.3 us (21%)
  local copies, waits for them, and re-layouts  57.2 us (20%)
  blocking collectives  32.8 us (12%)
  matrix products  28.1 us (10%)
  other arithmetic  19.4 us (7%)
  between operations  15.3 us (5%)
    all_to_all x1, waiting for transfers between devices, shards(): lax.all_to_all(outgoing, 'blk', split_axis=2, concat_axis=2, tiled=True)  38.7 us
    psum x1, blocking collectives, shards(): lax.psum((jnp.sum(floats, axis=1), jnp.sum(floats * floats, axis=1)), 'he...  19.7 us
    slice x2, local copies, waits for them, and re-layouts, shards(): cached_values = blocks_in[1].reshape(heads_here, HD, -1).astype(jnp.float32)  19.6 us
    all_to_all x1, starting transfers between devices, shards(): lax.all_to_all(labels, 'blk', split_axis=2, concat_axis=2, tiled=True)  15.2 us
    dot_general x2, matrix products, softmax_part(): jnp.einsum('hqk,hdk->hdq', expo, values, precision=lax.Precision.HIGHEST)  14.7 us
    ppermute x3, starting transfers between devices, product_in_turn(): from_right = lax.ppermute(from_right, axis, left)  13.3 us
    psum x1, blocking collectives, shards(): square_sums = lax.psum(jnp.sum(row_floats * row_floats, axis=0), 'head')  13.1 us
    all_to_all x1, starting transfers between devices, shards(): lax.all_to_all(starts, 'blk', split_axis=0, concat_axis=0, tiled=True)  11.6 us
  transfers between devices with their start and end apart: 12, of which 8 were waited for; matrix products, arithmetic and copies ran while one was open for 18% of the time, Pallas kernels for 0%

profile of v1, /device:TPU:1, one launch (start us, length us, event | category | flops | bytes accessed | tf_op | source)
XLA Modules:
  0.0 281.8 jit_solution(16765341290492751347)
XLA Ops:
  8.8 11.6 %all-to-all-start.2 = ((s32[64,1,1]{2,1,0:T(1,128)}), s32[64,1,1]{2,1,0:T(1,128)S(1)}, u32[]{:S(2)}, u32[]{:S(2)}) async-start(s32[64,1,1]{2,1,0:T(1,128)} %copy.44), calls=%async_computation.2 | async-start | bytes 65536 | tf_op jit(solution)/shard_map/all_to_all | solution.py:120
  21.5 19.7 %all-reduce = (f32[4,128]{1,0:T(4,128)S(1)}, f32[4,128]{1,0:T(4,128)S(1)}) all-reduce(f32[4,128]{1,0:T(4,128)S(1)} %get-tuple-element.23, f32[4,128]{1,0:T(4,128)S(1)} %get-tuple-element.22), channel_id=1, replica_groups=mesh['head'=8,'blk'=64] {'head'}, use_global_device_ids=true, to_apply=%region_11.12 | all-reduce | flops 1024 | bytes 8192 | tf_op jit(solution)/shard_map/psum | solution.py:83
  44.3 2.4 copy.38
  50.9 4.9 %convert_bitcast_fusion = bf16[2,176,128,32]{2,1,3,0:T(8,128)(2,1)} fusion(bf16[2,176,64,32]{1,3,2,0:T(8,128)(2,1)} %bitcast.63, s32[64]{0:T(128)S(1)} %get-tuple-element.61, pred[64]{0:T(512)(128)(4,1)S(1)} %get-tuple-element.24), kind=kOutput, calls=%fused_computation.13 | convolution fusion | flops 186007552 | bytes 4325696 | tf_op jit(solution)/shard_map/wo,cfob->cfwb/dot_general | solution.py:190
  57.2 7.6 %copy.40 = bf16[2,176,128,32]{1,3,2,0:T(8,128)(2,1)} copy(bf16[2,176,128,32]{2,1,3,0:T(8,128)(2,1)} %convert_bitcast_fusion) | data formatting | bytes 5767168 | tf_op jit(solution)/shard_map/convert_element_type | solution.py:192
  64.8 10.1 %copy.41 = bf16[2,176,4096]{1,0,2:T(2,128)(2,1)} copy(bf16[2,176,4096]{1,2,0:T(8,128)(2,1)} %bitcast.62) | data formatting | bytes 5767168 | tf_op jit(solution)/shard_map/reshape | solution.py:193
  74.9 5.5 %reduce-scatter.4.cloned.1.call-done = f32[176,128]{1,0:T(8,128)} async-done(((f32[1408,128]{1,0:T(8,128)}), f32[176,128]{1,0:T(8,128)}) %reduce-scatter.4.cloned.1.call-update) | async-done | bytes 90128
  81.6 15.2 %all-to-all-start.1 = ((s32[1,1,128]{1,0,2:T(1,128)}), s32[1,1,128]{1,0,2:T(1,128)S(1)}, u32[]{:S(2)}, u32[]{:S(2)}) async-start(s32[1,1,128]{1,0,2:T(1,128)} %copy.43), calls=%async_computation.1 | async-start | bytes 131072 | tf_op jit(solution)/shard_map/all_to_all | solution.py:198
  97.9 8.7 %all-to-all-done.1 = s32[1,1,128]{1,0,2:T(1,128)S(1)} async-done(((s32[1,1,128]{1,0,2:T(1,128)}), s32[1,1,128]{1,0,2:T(1,128)S(1)}, u32[]{:S(2)}, u32[]{:S(2)}) %all-to-all-start.1) | async-done | bytes 544 | tf_op jit(solution)/shard_map/all_to_all | solution.py:198
  106.6 4.4 %all-to-all-start.3 = ((bf16[64,4,176]{2,1,0:T(4,128)(2,1)}), bf16[64,4,176]{2,1,0:T(4,128)(2,1)S(1)}, u32[]{:S(2)}, u32[]{:S(2)}) async-start(bf16[64,4,176]{2,1,0:T(4,128)(2,1)} %reshape.266), calls=%async_computation.3 | async-start | bytes 262144 | tf_op jit(solution)/shard_map/all_to_all | solution.py:119
  111.1 10.4 %all-to-all-done.3 = bf16[64,4,176]{2,1,0:T(4,128)(2,1)S(1)} async-done(((bf16[64,4,176]{2,1,0:T(4,128)(2,1)}), bf16[64,4,176]{2,1,0:T(4,128)(2,1)S(1)}, u32[]{:S(2)}, u32[]{:S(2)}) %all-to-all-start.3) | async-done | bytes 90144 | tf_op jit(solution)/shard_map/all_to_all | solution.py:119
  121.5 5.6 %all-to-all-start = ((bf16[2,176,4096]{1,0,2:T(2,128)(2,1)}), bf16[2,176,4096]{1,0,2:T(2,128)(2,1)}, u32[]{:S(2)}, u32[]{:S(2)}) async-start(bf16[2,176,4096]{1,0,2:T(2,128)(2,1)} %copy.41), calls=%async_computation | async-start | bytes 8388608 | tf_op jit(solution)/shard_map/all_to_all | solution.py:197
  135.8 13.1 %psum.23 = f32[512]{0:T(512)S(1)} all-reduce(f32[512]{0:T(512)S(1)} %get-tuple-element.55), channel_id=1, replica_groups=mesh['head'=8,'blk'=64] {'head'}, use_global_device_ids=true, to_apply=%region_14.15 | all-reduce | flops 512 | bytes 4096 | tf_op jit(solution)/shard_map/psum | solution.py:134
  151.4 4.1 %collective-permute-start = (bf16[176,512]{1,0:T(8,128)(2,1)S(1)}, bf16[176,512]{1,0:T(8,128)(2,1)S(1)}, u32[]{:S(2)}, u32[]{:S(2)}) collective-permute-start(bf16[176,512]{1,0:T(8,128)(2,1)S(1)} %multiply_convert_fusion), channel_id=1, source_target_pairs={{0,448},{64,0},{128,64},{192,128},{256,192},{320,256},{384,320},{4... | collective-permute-start | bytes 540680 | tf_op jit(solution)/shard_map/ppermute | solution.py:23
  158.7 4.6 %collective-permute-start.2 = (bf16[176,512]{1,0:T(8,128)(2,1)S(1)}, bf16[176,512]{1,0:T(8,128)(2,1)S(1)}, u32[]{:S(2)}, u32[]{:S(2)}) collective-permute-start(bf16[176,512]{1,0:T(8,128)(2,1)S(1)} %collective-permute-done), channel_id=1, source_target_pairs={{0,448},{64,0},{128,64},{192,128},{256,192},{320,256},{384,320},{4... | collective-permute-start | bytes 540680 | tf_op jit(solution)/shard_map/ppermute | solution.py:23
  166.6 4.6 %collective-permute-start.4 = (bf16[176,512]{1,0:T(8,128)(2,1)S(1)}, bf16[176,512]{1,0:T(8,128)(2,1)S(1)}, u32[]{:S(2)}, u32[]{:S(2)}) collective-permute-start(bf16[176,512]{1,0:T(8,128)(2,1)S(1)} %collective-permute-done.2), channel_id=1, source_target_pairs={{0,448},{64,0},{128,64},{192,128},{256,192},{320,256},{384,320},{4... | collective-permute-start | bytes 540680 | tf_op jit(solution)/shard_map/ppermute | solution.py:23
  175.2 5.2 %collective-permute-done.6 = bf16[176,512]{1,0:T(8,128)(2,1)S(1)} collective-permute-done((bf16[176,512]{1,0:T(8,128)(2,1)S(1)}, bf16[176,512]{1,0:T(8,128)(2,1)S(1)}, u32[]{:S(2)}, u32[]{:S(2)}) %collective-permute-start.6) | collective-permute-done | bytes 180256 | tf_op jit(solution)/shard_map/ppermute | solution.py:21
  184.4 38.7 %all-to-all-done = bf16[2,176,4096]{1,0,2:T(2,128)(2,1)} async-done(((bf16[2,176,4096]{1,0,2:T(2,128)(2,1)}), bf16[2,176,4096]{1,0,2:T(2,128)(2,1)}, u32[]{:S(2)}, u32[]{:S(2)}) %all-to-all-start) | async-done | bytes 2883616 | tf_op jit(solution)/shard_map/all_to_all | solution.py:197
  223.1 9.8 %fusion.90 = (bf16[1,176,4096]{1,0,2:T(2,128)(2,1)}, bf16[1,176,4096]{1,0,2:T(2,128)(2,1)}) fusion(bf16[2,176,4096]{1,0,2:T(2,128)(2,1)} %all-to-all-done), kind=kLoop, calls=%fused_computation.149 | loop fusion | bytes 5767168 | tf_op jit(solution)/shard_map/slice | solution.py:201
  232.9 9.8 %copy.42 = bf16[1,176,4096]{2,1,0:T(8,128)(2,1)S(1)} copy(bf16[1,176,4096]{1,0,2:T(2,128)(2,1)} %get-tuple-element.41) | data formatting | bytes 2883584 | tf_op jit(solution)/shard_map/slice | solution.py:201
  242.7 9.8 %copy.45 = bf16[1,176,4096]{2,1,0:T(8,128)(2,1)S(1)} copy(bf16[1,176,4096]{1,0,2:T(2,128)(2,1)} %get-tuple-element.42) | data formatting | bytes 2883584 | tf_op jit(solution)/shard_map/slice | solution.py:200
  252.5 2.8 %fusion = (f32[2,512]{1,0:T(2,128)S(1)}, f32[2,512,4096]{2,1,0:T(8,128)S(1)}) fusion(pred[4096]{0:T(1024)(128)(4,1)S(1)} %and.92, bf16[2,88,4096]{2,1,0:T(8,128)(2,1)S(1)} %bitcast.64, bf16[2,44,512]{2,1,0:T(8,128)(2,1)S(1)} %copy-done.9, bf16[2,44,512]{2,1,0:T(8,128)(2,1)S(1)} %get-tuple-element.45), kind=kOutput, calls=%fused_computation.2 | convolution fusion | flops 751139840 | bytes 18407424 | tf_op jit(solution)/shard_map/while/body/eval_jaxpr/hdq,hdk->hqk/dot_general | solution.py:45
  255.4 4.9 %fusion.1 = f32[2,512]{1,0:T(2,128)S(1)} fusion(f32[2,512,4096]{2,1,0:T(8,128)S(1)} %get-tuple-element.60, f32[2,512]{1,0:T(2,128)S(1)} %get-tuple-element.59, pred[4096]{0:T(1024)(128)(4,1)S(1)} %and.92), kind=kLoop, calls=%fused_computation.3 | loop fusion | flops 20970496 | bytes 16789504 | tf_op jit(solution)/shard_map/while/body/eval_jaxpr/reduce_sum | solution.py:50
  261.8 13.2 %fusion.26 = bf16[2,88,512]{2,1,0:T(8,128)(2,1)} fusion(f32[2,88,512]{2,1,0:T(8,128)S(1)} %fusion.17, bf16[2,88,4096]{2,1,0:T(8,128)(2,1)S(1)} %bitcast.67, f32[2,512,4096]{2,1,0:T(8,128)S(1)} %get-tuple-element.60, f32[2,512]{1,0:T(2,128)S(1)} %get-tuple-element.59, pred[4096]{0:T(1024)(128)(4,1)S(1)} %and.92, f32[2,512]{1,0:T(2,128)S(1)} %get-tuple-element.28, ...), kind=kOutput, calls=%fused_computation.43 | convolution fusion | flops 4446322688 | bytes 18776064 | tf_op jit(solution)/shard_map/while/body/eval_jaxpr/hqk,hdk->hdq/dot_general | solution.py:51
  (96 shorter events, 39.7 us)
Async XLA Ops:
  7.2 34.0 %copy-start = (bf16[4,176,1408]{2,1,0:T(8,128)(2,1)S(1)}, bf16[4,176,1408]{2,1,0:T(8,128)(2,1)}, u32[]{:S(2)}) copy-start(bf16[4,176,1408]{2,1,0:T(8,128)(2,1)} %param.12) | copy-start | bytes 5947396
  8.8 72.8 %all-to-all-start.2 = ((s32[64,1,1]{2,1,0:T(1,128)}), s32[64,1,1]{2,1,0:T(1,128)S(1)}, u32[]{:S(2)}, u32[]{:S(2)}) async-start(s32[64,1,1]{2,1,0:T(1,128)} %copy.44), calls=%async_computation.2 | async-start | bytes 65536 | tf_op jit(solution)/shard_map/all_to_all | solution.py:120
  20.4 60.0 %reduce-scatter.4.cloned.1.call-start = ((), (), s32[]{:S(2)}) async-start(), calls=%async_computation.5 | async-start | bytes 811008
  42.7 1.6 copy-start.5
  43.9 2.8 %copy-start.10 = (s32[64,128]{1,0:T(8,128)S(1)}, s32[64,128]{1,0:T(8,128)}, u32[]{:S(2)}) copy-start(s32[64,128]{1,0:T(8,128)} %param.18) | copy-start | bytes 98308
  81.6 25.0 %all-to-all-start.1 = ((s32[1,1,128]{1,0,2:T(1,128)}), s32[1,1,128]{1,0,2:T(1,128)S(1)}, u32[]{:S(2)}, u32[]{:S(2)}) async-start(s32[1,1,128]{1,0,2:T(1,128)} %copy.43), calls=%async_computation.1 | async-start | bytes 131072 | tf_op jit(solution)/shard_map/all_to_all | solution.py:198
  106.6 14.9 %all-to-all-start.3 = ((bf16[64,4,176]{2,1,0:T(4,128)(2,1)}), bf16[64,4,176]{2,1,0:T(4,128)(2,1)S(1)}, u32[]{:S(2)}, u32[]{:S(2)}) async-start(bf16[64,4,176]{2,1,0:T(4,128)(2,1)} %reshape.266), calls=%async_computation.3 | async-start | bytes 262144 | tf_op jit(solution)/shard_map/all_to_all | solution.py:119
  111.1 24.3 %copy-start.11 = (bf16[176,512]{1,0:T(8,128)(2,1)S(1)}, bf16[176,512]{1,0:T(8,128)(2,1)}, u32[]{:S(2)}) copy-start(bf16[176,512]{1,0:T(8,128)(2,1)} %param.14) | copy-start | bytes 540676
  121.5 101.6 %all-to-all-start = ((bf16[2,176,4096]{1,0,2:T(2,128)(2,1)}), bf16[2,176,4096]{1,0,2:T(2,128)(2,1)}, u32[]{:S(2)}, u32[]{:S(2)}) async-start(bf16[2,176,4096]{1,0,2:T(2,128)(2,1)} %copy.41), calls=%async_computation | async-start | bytes 8388608 | tf_op jit(solution)/shard_map/all_to_all | solution.py:197
  127.2 28.3 %copy-start.2 = (bf16[3,176,1408]{2,1,0:T(8,128)(2,1)S(1)}, bf16[3,176,1408]{2,1,0:T(8,128)(2,1)}, u32[]{:S(2)}) copy-start(bf16[3,176,1408]{2,1,0:T(8,128)(2,1)} %param.16) | copy-start | bytes 4460548
  149.0 7.8 %collective-permute-start.1 = (bf16[176,512]{1,0:T(8,128)(2,1)S(1)}, bf16[176,512]{1,0:T(8,128)(2,1)S(1)}, u32[]{:S(2)}, u32[]{:S(2)}) collective-permute-start(bf16[176,512]{1,0:T(8,128)(2,1)S(1)} %multiply_convert_fusion), channel_id=1, source_target_pairs={{0,64},{64,128},{128,192},{192,256},{256,320},{320,384},{384,448},... | collective-permute-start | bytes 540680 | tf_op jit(solution)/shard_map/ppermute | solution.py:21
  151.4 7.4 %collective-permute-start = (bf16[176,512]{1,0:T(8,128)(2,1)S(1)}, bf16[176,512]{1,0:T(8,128)(2,1)S(1)}, u32[]{:S(2)}, u32[]{:S(2)}) collective-permute-start(bf16[176,512]{1,0:T(8,128)(2,1)S(1)} %multiply_convert_fusion), channel_id=1, source_target_pairs={{0,448},{64,0},{128,64},{192,128},{256,192},{320,256},{384,320},{4... | collective-permute-start | bytes 540680 | tf_op jit(solution)/shard_map/ppermute | solution.py:23
  156.8 7.8 %collective-permute-start.3 = (bf16[176,512]{1,0:T(8,128)(2,1)S(1)}, bf16[176,512]{1,0:T(8,128)(2,1)S(1)}, u32[]{:S(2)}, u32[]{:S(2)}) collective-permute-start(bf16[176,512]{1,0:T(8,128)(2,1)S(1)} %collective-permute-done.1), channel_id=1, source_target_pairs={{0,64},{64,128},{128,192},{192,256},{256,320},{320,384},{384,448},... | collective-permute-start | bytes 540680 | tf_op jit(solution)/shard_map/ppermute | solution.py:21
  158.7 7.8 %collective-permute-start.2 = (bf16[176,512]{1,0:T(8,128)(2,1)S(1)}, bf16[176,512]{1,0:T(8,128)(2,1)S(1)}, u32[]{:S(2)}, u32[]{:S(2)}) collective-permute-start(bf16[176,512]{1,0:T(8,128)(2,1)S(1)} %collective-permute-done), channel_id=1, source_target_pairs={{0,448},{64,0},{128,64},{192,128},{256,192},{320,256},{384,320},{4... | collective-permute-start | bytes 540680 | tf_op jit(solution)/shard_map/ppermute | solution.py:23
  164.7 7.8 %collective-permute-start.5 = (bf16[176,512]{1,0:T(8,128)(2,1)S(1)}, bf16[176,512]{1,0:T(8,128)(2,1)S(1)}, u32[]{:S(2)}, u32[]{:S(2)}) collective-permute-start(bf16[176,512]{1,0:T(8,128)(2,1)S(1)} %collective-permute-done.3), channel_id=1, source_target_pairs={{0,64},{64,128},{128,192},{192,256},{256,320},{320,384},{384,448},... | collective-permute-start | bytes 540680 | tf_op jit(solution)/shard_map/ppermute | solution.py:21
  166.6 8.2 %collective-permute-start.4 = (bf16[176,512]{1,0:T(8,128)(2,1)S(1)}, bf16[176,512]{1,0:T(8,128)(2,1)S(1)}, u32[]{:S(2)}, u32[]{:S(2)}) collective-permute-start(bf16[176,512]{1,0:T(8,128)(2,1)S(1)} %collective-permute-done.2), channel_id=1, source_target_pairs={{0,448},{64,0},{128,64},{192,128},{256,192},{320,256},{384,320},{4... | collective-permute-start | bytes 540680 | tf_op jit(solution)/shard_map/ppermute | solution.py:23
  172.5 7.8 %collective-permute-start.6 = (bf16[176,512]{1,0:T(8,128)(2,1)S(1)}, bf16[176,512]{1,0:T(8,128)(2,1)S(1)}, u32[]{:S(2)}, u32[]{:S(2)}) collective-permute-start(bf16[176,512]{1,0:T(8,128)(2,1)S(1)} %collective-permute-done.5), channel_id=1, source_target_pairs={{0,64},{64,128},{128,192},{192,256},{256,320},{320,384},{384,448},... | collective-permute-start | bytes 540680 | tf_op jit(solution)/shard_map/ppermute | solution.py:21
  180.7 1.7 copy-start.6
  181.8 2.6 copy-start.8
  182.4 1.4 copy-start.3
  242.7 9.8 %copy-start.9 = (bf16[2,44,512]{2,1,0:T(8,128)(2,1)S(1)}, bf16[2,44,512]{2,1,0:T(8,128)(2,1)}, u32[]{:S(2)}) copy-start(bf16[2,44,512]{2,1,0:T(8,128)(2,1)} %copy-done.8) | copy-start | bytes 270340
  255.3 4.9 %copy-start.4 = (f32[2,512,512]{1,2,0:T(8,128)S(1)}, f32[2,512,512]{1,2,0:T(8,128)}, u32[]{:S(2)}) copy-start(f32[2,512,512]{1,2,0:T(8,128)} %copy-done.3) | copy-start | bytes 6291460
  255.4 4.9 %copy-start.7 = (bf16[1,176,512]{2,1,0:T(8,128)(2,1)S(1)}, bf16[1,176,512]{2,1,0:T(8,128)(2,1)}, u32[]{:S(2)}) copy-start(bf16[1,176,512]{2,1,0:T(8,128)(2,1)} %copy-done.6) | copy-start | bytes 540676
  261.8 13.2 %copy-start.1 = (bf16[4,176,1408]{2,1,0:T(8,128)(2,1)S(1)}, bf16[4,176,1408]{2,1,0:T(8,128)(2,1)}, u32[]{:S(2)}) copy-start(bf16[4,176,1408]{2,1,0:T(8,128)(2,1)} %param.12) | copy-start | bytes 5947396
Sparse Core Ops, SparseCore 0:
  44.1 36.3 reduce-scatter.3
